TPU v7x, 128 devices: a whole 4x4x4 slice. The times are simulated.
128 devices in a mesh: snap: 4 (over z_lo, core), pts: 32 (over z_hi, x, y).
Axes of the slice: x: 4, y: 4, z: 4 (z_hi: 2, z_lo: 2; z = z_hi * 2 + z_lo), core: 2. Of those that a mesh axis runs over, the one named last changes fastest.
Arguments:
- strains: bfloat16 [6, 512, 131072], P(None, 'snap', 'pts'), may hold values from -3 to 3
- moduli: float32 [2, 131072], P(None, 'pts'), may hold values from 0.5 to 2
- range_test: bfloat16 [131072, 256], P('pts'), may hold values from -0.015625 to 0.015625
- corange_test: bfloat16 [256, 512], replicated, may hold values from -0.25 to 0.25
- core_left: float32 [512, 512], P(None, 'snap'), may hold values from -0.25 to 0.25
- core_right: bfloat16 [512, 131072], P(None, 'pts'), may hold values from -0.015625 to 0.015625
Outputs:
- range_sketch: float32 [512, 256], P('snap')
- corange_sketch: float32 [256, 131072], P('snap', 'pts')
- core_sketch: float32 [512, 512], replicated
All inputs are finite; a program needn't handle non-finite values.
Results may differ from a plain program's by a relative error of at most 0.0031.
Values may be sent and summed in bfloat16 or wider, within the bound.
A program may use at most 64 MiB of HBM per device.

v0:
```python
import math

import jax
import jax.numpy as jnp
from jax import lax
from jax.sharding import PartitionSpec as P


def energy_field(strains, moduli):
    strain_xx = strains[0].astype(jnp.float32)
    strain_yy = strains[1].astype(jnp.float32)
    strain_zz = strains[2].astype(jnp.float32)
    strain_xy = strains[3].astype(jnp.float32)
    strain_yz = strains[4].astype(jnp.float32)
    strain_xz = strains[5].astype(jnp.float32)
    lame_first = moduli[0][None, :]
    shear_mod = moduli[1][None, :]
    strain_trace = strain_xx + strain_yy + strain_zz
    mean_strain = strain_trace / 3.0
    dev_xx = strain_xx - mean_strain
    dev_yy = strain_yy - mean_strain
    dev_zz = strain_zz - mean_strain
    dev_square = (
        dev_xx * dev_xx
        + dev_yy * dev_yy
        + dev_zz * dev_zz
        + 2.0 * (strain_xy * strain_xy + strain_yz * strain_yz + strain_xz * strain_xz)
    ) / 6.0
    dev_norm = jnp.sqrt(dev_square)
    dev_det = (
        dev_xx * (dev_yy * dev_zz - strain_yz * strain_yz)
        - strain_xy * (strain_xy * dev_zz - strain_yz * strain_xz)
        + strain_xz * (strain_xy * strain_yz - dev_yy * strain_xz)
    )
    sine_part = jnp.sqrt(
        jnp.maximum(4.0 * dev_square * dev_square * dev_square - dev_det * dev_det, 0.0)
    )
    angle_third = jnp.arctan2(sine_part, dev_det) / 3.0
    positive_trace = jnp.maximum(strain_trace, 0.0)
    density = 0.5 * lame_first * positive_trace * positive_trace
    for order in range(3):
        principal = mean_strain + 2.0 * dev_norm * jnp.cos(
            angle_third - 2.0 * math.pi * order / 3.0
        )
        positive = jnp.maximum(principal, 0.0)
        density = density + shear_mod * positive * positive
    return density.astype(jnp.bfloat16)


def per_device(strains, moduli, range_test, corange_test, core_left, core_right):
    energy = energy_field(strains, moduli)
    snap_rows = energy.shape[0]
    range_part = jnp.dot(energy, range_test, preferred_element_type=jnp.float32)
    cross_part = lax.dot_general(
        energy, core_right, (((1,), (1,)), ((), ())), preferred_element_type=jnp.float32
    )
    range_sketch = lax.psum(range_part, "pts")
    core_share = jnp.dot(core_left, cross_part, precision=lax.Precision.HIGHEST)
    core_sketch = lax.psum(core_share, ("snap", "pts"))
    own_cols = lax.dynamic_slice_in_dim(
        corange_test, lax.axis_index("snap") * snap_rows, snap_rows, 1
    )
    corange_sketch = lax.psum_scatter(
        jnp.dot(own_cols, energy, preferred_element_type=jnp.float32),
        "snap",
        scatter_dimension=0,
        tiled=True,
    )
    return (range_sketch, corange_sketch, core_sketch)


def solution(mesh):
    in_specs = (
        P(None, "snap", "pts"),
        P(None, "pts"),
        P("pts", None),
        P(),
        P(None, "snap"),
        P(None, "pts"),
    )
    out_specs = (P("snap", None), P("snap", "pts"), P())
    return jax.shard_map(
        per_device, mesh=mesh, in_specs=in_specs, out_specs=out_specs, check_vma=False
    )
```

profile of v0, /device:TPU:0, one launch (start us, length us, event | category | flops | bytes accessed | tf_op | source)
XLA Modules:
  0.0 557.0 jit_solution(8219614878723953401)
XLA Ops:
  8.0 0.0 copy-start
  8.0 0.0 all-reduce.5.cloned.1.call-start
  8.1 0.9 slice_multiply_fusion
  9.0 0.0 copy-start.1
  9.0 31.8 %fusion.11 = bf16[128,4096]{1,0:T(8,128)(2,1)S(1)} fusion(bf16[6,128,4096]{2,1,0:T(8,128)(2,1)} %param.6, f32[4096]{0:T(1024)S(1)} %bitcast.30, f32[4096]{0:T(1024)S(1)} %bitcast.29), kind=kLoop, calls=%fused_computation.30 | loop fusion | flops 36700160 | bytes 7372800 | tf_op jit(solution)/shard_map/convert_element_type | solution.py:47
  40.9 0.0 copy-done.1
  40.9 0.0 copy-start.2
  40.9 1.5 fusion.27
  42.4 0.0 copy-done.2
  42.4 2.0 convolution_bitcast_fusion
  44.4 0.0 all-reduce.5.cloned.1.call-update
  44.5 0.0 all-reduce.3.cloned.1.call-start
  44.5 0.0 copy-done
  44.5 1.1 fusion.26
  45.6 0.0 all-reduce.3.cloned.1.call-update
  45.7 0.0 reduce-scatter.2.cloned.1.call-start
  45.7 3.5 fusion.23
  49.2 0.0 reduce-scatter.2.cloned.1.call-update
  49.2 170.6 %all-reduce.5.cloned.1.call-done = f32[512,512]{0,1:T(8,128)} async-done(((f32[512,512]{0,1:T(8,128)}), f32[512,512]{0,1:T(8,128)}) %all-reduce.5.cloned.1.call-update) | async-done | bytes 1048592 | tf_op jit(solution)/shard_map/psum | solution.py:59
  219.8 2.5 copy.9
  222.3 325.7 %all-reduce.3.cloned.1.call-done = f32[128,256]{1,0:T(8,128)} async-done(((f32[128,256]{1,0:T(8,128)}), f32[128,256]{1,0:T(8,128)}) %all-reduce.3.cloned.1.call-update) | async-done | bytes 131088 | tf_op jit(solution)/shard_map/psum | solution.py:57
  548.0 0.0 reduce-scatter.2.cloned.1.call-done
  548.0 1.6 copy.12
Async XLA Ops:
  8.0 36.5 %copy-start = (bf16[4096,256]{1,0:T(8,128)(2,1)S(1)}, bf16[4096,256]{1,0:T(8,128)(2,1)}, u32[]{:S(2)}) copy-start(bf16[4096,256]{1,0:T(8,128)(2,1)} %param.8) | copy-start | bytes 6291460
  8.0 211.8 %all-reduce.5.cloned.1.call-start = ((), (), s32[]{:S(2)}) async-start(), calls=%async_computation.3 | async-start | bytes 2097152 | tf_op jit(solution)/shard_map/psum | solution.py:59
  9.0 31.9 %copy-start.1 = (bf16[512,4096]{1,0:T(8,128)(2,1)S(1)}, bf16[512,4096]{1,0:T(8,128)(2,1)}, u32[]{:S(2)}) copy-start(bf16[512,4096]{1,0:T(8,128)(2,1)} %param.11) | copy-start | bytes 12582916
  40.9 1.6 copy-start.2
  44.5 503.6 %all-reduce.3.cloned.1.call-start = ((), (), s32[]{:S(2)}) async-start(), calls=%async_computation.1 | async-start | bytes 262144 | tf_op jit(solution)/shard_map/psum | solution.py:57
  45.7 502.4 %reduce-scatter.2.cloned.1.call-start = ((), (), s32[]{:S(2)}) async-start(), calls=%async_computation.2 | async-start | bytes 5242880 | tf_op jit(solution)/shard_map/reduce_scatter | solution.py:63
Sparse Core Ops, SparseCore 0:
  44.6 175.1 all-reduce.4
  222.8 325.1 all-reduce.2
Sparse Core Ops, SparseCore 1:
  49.3 47.8 reduce-scatter.1
where the time goes:
time: 557 us
  waiting for transfers between devices  496 us (89%)
  other arithmetic  32.8 us (6%)
  between operations  15.6 us (3%)
  matrix products  8.11 us (1%)
    psum x1, waiting for transfers between devices, per_device(): range_sketch = lax.psum(range_part, 'pts')  326 us
    psum x1, waiting for transfers between devices, per_device(): core_sketch = lax.psum(core_share, ('snap', 'pts'))  171 us
    convert_element_type x1, other arithmetic, energy_field(): return density.astype(jnp.bfloat16)  31.8 us
  transfers between devices with their start and end apart: 3, of which 2 were waited for; matrix products, arithmetic and copies ran while one was open for 1% of the time, Pallas kernels for 0%

commit v1 on v0

v1 whole, which is shorter than its diff:
```python
import jax
import jax.numpy as jnp
from jax import lax
from jax.experimental import pallas as pl
from jax.experimental.pallas import tpu as pltpu
from jax.sharding import PartitionSpec as P

MESH = pl.DeviceIdType.MESH
F32 = jnp.float32
BF16 = jnp.bfloat16
NT = (((1,), (1,)), ((), ()))

CHUNK = 512
LANES = 128
ROWS = 16

ROOT = (
    0.5000000055642606,
    0.24999799048045115,
    -0.18738033617581623,
    0.24724082978273138,
    -0.37786422526526064,
    0.5312551787148476,
    -0.5329691265664762,
    0.26064257700530713,
)
TINY = 1e-36

FAR = sorted(
    ((dx, dy) for dx in range(4) for dy in range(4) if (dx, dy) != (0, 0)),
    key=lambda d: -(min(d[0], 4 - d[0]) + min(d[1], 4 - d[1])),
)
COLUMN = [(2, 0), (2, 1), (1, 0), (3, 0), (1, 1), (3, 1), (0, 1)]


def energy_tile(xx, yy, zz, xy, yz, xz, half_lame, shear):
    trace = xx + yy + zz
    mean = trace * (1.0 / 3.0)
    a = xx - mean
    b = yy - mean
    c = zz - mean
    ac = a * c
    d2 = xy * xy
    e2 = yz * yz
    f2 = xz * xz
    j2 = (b * b - ac) + ((d2 + e2) + f2)
    de = xy * yz
    half_det = 0.5 * (b * (ac - f2) - a * e2 - c * d2) + de * xz
    inv = lax.rsqrt(jnp.maximum(j2, TINY))
    norm = j2 * inv
    ratio = (jnp.abs(half_det) * inv) * (inv * inv)
    ratio = ratio + ratio
    root = jnp.full_like(ratio, ROOT[-1])
    for coef in ROOT[-2::-1]:
        root = root * ratio + coef
    outer = norm * root
    rest = jnp.maximum(j2 - 3.0 * (outer * outer), 0.0)
    split = rest * lax.rsqrt(jnp.maximum(rest, TINY))
    outer = jnp.where(half_det < 0.0, -outer, outer)
    lone = jnp.maximum(mean + (outer + outer), 0.0)
    middle = mean - outer
    upper = jnp.maximum(middle + split, 0.0)
    lower = jnp.maximum(middle - split, 0.0)
    squares = lone * lone + upper * upper + lower * lower
    positive = jnp.maximum(trace, 0.0)
    return half_lame * (positive * positive) + shear * squares


def kernel(
    strains_hbm, moduli_hbm, range_hbm, corange_hbm, left_hbm, right_hbm,
    own_hbm, range_out_hbm, core_out_hbm,
    strains, moduli, range_w, right_w, corange_w, left_w, energy,
    cross_acc, range_acc, own_acc, far_acc, pair_send, pair_recv, far_send, far_recv,
    cross_send, cross_recv, range_recv, range_mid, range_zrecv, range_fin, range_all,
    col_send, col_recv, col_piece, col_all, core_all,
    in_sems, w_sems, pair_ssem, pair_rsem, far_ssem, far_rsem,
    plane_sems, range_sems, col_sems, out_sems,
):
    snap = lax.axis_index("snap")
    pts = lax.axis_index("pts")
    z_lo = snap // 2
    core = snap % 2
    z_hi = pts // 16
    x = (pts // 4) % 4
    y = pts % 4
    z = z_hi * 2 + z_lo
    plane = pts % 16
    slot = z * 2 + core

    def in_plane(dx, dy):
        return (x + dx) % 4 * 4 + (y + dy) % 4

    def plane_id(xy):
        return {"snap": snap, "pts": z_hi * 16 + xy}

    def in_column(dz, dc):
        return (z + dz) % 4 * 2 + (core + dc) % 2

    def column_id(q):
        zz = q // 2
        return {"snap": zz % 2 * 2 + q % 2, "pts": zz // 2 * 16 + plane}

    pair = {"snap": z_lo * 2 + (1 - core), "pts": pts}
    far = {"snap": (1 - z_lo) * 2 + core, "pts": pts}

    chunks = strains.shape[0]

    def inputs(j):
        cols = pl.ds(pl.multiple_of(j * CHUNK, CHUNK), CHUNK)
        return (
            pltpu.make_async_copy(strains_hbm.at[:, :, cols], strains.at[j], in_sems.at[0, j]),
            pltpu.make_async_copy(moduli_hbm.at[:, cols], moduli.at[j], in_sems.at[1, j]),
            pltpu.make_async_copy(right_hbm.at[:, cols], right_w.at[j], in_sems.at[2, j]),
            pltpu.make_async_copy(range_hbm.at[cols, :], range_w.at[j], in_sems.at[3, j]),
        )

    weights = []
    own_cols = pl.ds(pl.multiple_of(snap * 128, 128), 128)
    owners = (snap, (1 - z_lo) * 2 + core, z_lo * 2 + (1 - core), (1 - z_lo) * 2 + (1 - core))
    for n, owner in enumerate(owners):
        rows = pl.ds(pl.multiple_of(owner * 64, 64), 64)
        weights.append(
            pltpu.make_async_copy(
                corange_hbm.at[rows, own_cols], corange_w.at[pl.ds(n * 64, 64), :], w_sems.at[n]
            )
        )
    left_copy = pltpu.make_async_copy(left_hbm, left_w, w_sems.at[4])

    for copy in inputs(0):
        copy.start()
    for copy in weights:
        copy.start()

    @pl.loop(1, chunks)
    def _(j):
        for copy in inputs(j):
            copy.start()

    left_copy.start()

    barrier = pltpu.get_barrier_semaphore()
    for dx, dy in FAR:
        pl.semaphore_signal(
            barrier, inc=1, device_id=plane_id(in_plane(dx, dy)), device_id_type=MESH
        )
    for dz, dc in COLUMN:
        pl.semaphore_signal(
            barrier, inc=1, device_id=column_id(in_column(dz, dc)), device_id_type=MESH
        )

    cross_acc[...] = jnp.zeros_like(cross_acc)
    range_acc[...] = jnp.zeros_like(range_acc)
    for copy in weights:
        copy.wait()

    def pair_copy(j):
        return pltpu.make_async_remote_copy(
            src_ref=pair_send.at[j],
            dst_ref=pair_recv.at[j],
            send_sem=pair_ssem.at[j],
            recv_sem=pair_rsem.at[j],
            device_id=pair,
            device_id_type=MESH,
        )

    def far_copy(j):
        return pltpu.make_async_remote_copy(
            src_ref=far_send.at[j],
            dst_ref=far_recv.at[j],
            send_sem=far_ssem.at[j],
            recv_sem=far_rsem.at[j],
            device_id=far,
            device_id_type=MESH,
        )

    def pass_on(j):
        pair_copy(j).wait_recv()
        far_send[j] = (far_acc[j] + pair_recv[j, 1].astype(F32)).astype(BF16)
        far_copy(j).start()
        own_acc[j] = own_acc[j] + pair_recv[j, 0].astype(F32)

    @pl.loop(0, chunks)
    def _(j):
        for copy in inputs(j):
            copy.wait()

        @pl.loop(0, 128 // ROWS)
        def _(i):
            rows = pl.ds(pl.multiple_of(i * ROWS, ROWS), ROWS)
            for lane in range(0, CHUNK, LANES):
                cols = pl.ds(lane, LANES)
                parts = [strains[j, k, rows, cols].astype(F32) for k in range(6)]
                energy[rows, cols] = energy_tile(
                    *parts, 0.5 * moduli[j, 0:1, cols], moduli[j, 1:2, cols]
                ).astype(BF16)

        field = energy[...]
        own = jnp.dot(corange_w[...], field, preferred_element_type=F32)
        own_acc[j] = own[:64]
        far_acc[j] = own[64:128]
        pair_send[j, 0] = own[128:192].astype(BF16)
        pair_send[j, 1] = own[192:].astype(BF16)

        @pl.when(j == 0)
        def _():
            pl.semaphore_wait(barrier, len(FAR) + len(COLUMN))

        pair_copy(j).start()
        cross_acc[...] += lax.dot_general(right_w[j], field, NT, preferred_element_type=F32)
        range_acc[...] += jnp.dot(field, range_w[j], preferred_element_type=F32)

        @pl.when(j > 0)
        def _():
            pass_on(j - 1)

    for n in range(16):
        cross_send[n] = cross_acc[pl.ds(n * 32, 32), :].astype(BF16)
    plane_copies = []
    for n, (dx, dy) in enumerate(FAR):
        xy = in_plane(dx, dy)
        copy = pltpu.make_async_remote_copy(
            src_ref=cross_send.at[xy],
            dst_ref=cross_recv.at[n],
            send_sem=plane_sems.at[0],
            recv_sem=plane_sems.at[1],
            device_id=plane_id(xy),
            device_id_type=MESH,
        )
        copy.start()
    for n, (dx, dy) in enumerate(FAR):
        xy = in_plane(dx, dy)
        copy = pltpu.make_async_remote_copy(
            src_ref=range_acc.at[pl.ds(pl.multiple_of(xy * 8, 8), 8), :],
            dst_ref=range_recv.at[n],
            send_sem=range_sems.at[0],
            recv_sem=range_sems.at[1],
            device_id=plane_id(xy),
            device_id_type=MESH,
        )
        copy.start()

    pass_on(chunks - 1)
    left_copy.wait()

    def everything(ref, sems, device, send, recv):
        whole = pltpu.make_async_remote_copy(
            src_ref=ref,
            dst_ref=ref,
            send_sem=sems.at[send],
            recv_sem=sems.at[recv],
            device_id=device,
            device_id_type=MESH,
        )
        return whole

    some = plane_id(in_plane(1, 0))
    one = column_id(in_column(0, 1))

    everything(cross_recv, plane_sems, some, 0, 1).wait_recv()
    total = cross_acc[pl.ds(pl.multiple_of(plane * 32, 32), 32), :]
    for n in range(15):
        total = total + cross_recv[n].astype(F32)
    share = lax.dot_general(
        total, left_w[...], NT, precision=lax.Precision.HIGHEST, preferred_element_type=F32
    )
    for q in range(8):
        half, block = q // 4, q % 4
        col_send[q] = share[half * 16 : half * 16 + 16, block * 128 : block * 128 + 128]
    for n, (dz, dc) in enumerate(COLUMN):
        q = in_column(dz, dc)
        pltpu.make_async_remote_copy(
            src_ref=col_send.at[q],
            dst_ref=col_recv.at[n],
            send_sem=col_sems.at[0],
            recv_sem=col_sems.at[1],
            device_id=column_id(q),
            device_id_type=MESH,
        ).start()

    everything(range_recv, range_sems, some, 0, 1).wait_recv()
    part = range_acc[pl.ds(pl.multiple_of(plane * 8, 8), 8), :]
    for n in range(15):
        part = part + range_recv[n]
    range_mid[...] = part
    z_copy = pltpu.make_async_remote_copy(
        src_ref=range_mid,
        dst_ref=range_zrecv,
        send_sem=range_sems.at[2],
        recv_sem=range_sems.at[3],
        device_id=column_id(in_column(2, 0)),
        device_id_type=MESH,
    )
    z_copy.start()

    everything(col_recv, col_sems, one, 0, 1).wait_recv()
    piece = col_send[slot]
    for n in range(7):
        piece = piece + col_recv[n]
    col_piece[...] = piece.astype(BF16)
    for dz, dc in COLUMN:
        q = in_column(dz, dc)
        pltpu.make_async_remote_copy(
            src_ref=col_piece,
            dst_ref=col_all.at[slot],
            send_sem=col_sems.at[2],
            recv_sem=col_sems.at[3],
            device_id=column_id(q),
            device_id_type=MESH,
        ).start()
    mine = pltpu.make_async_copy(col_piece, col_all.at[slot], col_sems.at[3])
    mine.start()

    z_copy.wait_recv()
    range_fin[...] = part + range_zrecv[...]

    everything(col_all, col_sems, one, 2, 3).wait_recv()
    for dx, dy in FAR:
        pltpu.make_async_remote_copy(
            src_ref=col_all,
            dst_ref=core_all.at[plane],
            send_sem=plane_sems.at[2],
            recv_sem=plane_sems.at[3],
            device_id=plane_id(in_plane(dx, dy)),
            device_id_type=MESH,
        ).start()
    pltpu.make_async_copy(col_all, core_all.at[plane], plane_sems.at[3]).start()
    for dx, dy in FAR:
        pltpu.make_async_remote_copy(
            src_ref=range_fin,
            dst_ref=range_all.at[plane],
            send_sem=range_sems.at[4],
            recv_sem=range_sems.at[5],
            device_id=plane_id(in_plane(dx, dy)),
            device_id_type=MESH,
        ).start()
    pltpu.make_async_copy(range_fin, range_all.at[plane], range_sems.at[5]).start()

    def own_copy(j):
        cols = pl.ds(pl.multiple_of(j * CHUNK, CHUNK), CHUNK)
        return pltpu.make_async_copy(own_acc.at[j], own_hbm.at[:, cols], out_sems.at[j])

    @pl.loop(0, chunks)
    def _(j):
        far_copy(j).wait_recv()
        own_acc[j] = own_acc[j] + far_recv[j].astype(F32)
        own_copy(j).start()

    everything(range_all, range_sems, some, 4, 5).wait_recv()
    range_copy = pltpu.make_async_copy(range_all, range_out_hbm, out_sems.at[chunks])
    range_copy.start()
    everything(core_all, plane_sems, some, 2, 3).wait_recv()
    core_copy = pltpu.make_async_copy(core_all, core_out_hbm, out_sems.at[chunks + 1])
    core_copy.start()

    everything(cross_recv, plane_sems, some, 0, 1).wait_send()
    everything(range_recv, range_sems, some, 0, 1).wait_send()
    everything(range_mid, range_sems, some, 2, 3).wait_send()
    everything(col_recv, col_sems, one, 0, 1).wait_send()
    everything(col_all.at[pl.ds(0, 7)], col_sems, one, 2, 3).wait_send()
    everything(core_all.at[pl.ds(0, 15)], plane_sems, some, 2, 3).wait_send()
    everything(range_all.at[pl.ds(0, 15)], range_sems, some, 4, 5).wait_send()

    @pl.loop(0, chunks)
    def _(j):
        pair_copy(j).wait_send()
        far_copy(j).wait_send()
        own_copy(j).wait()

    range_copy.wait()
    core_copy.wait()


def per_device(strains, moduli, range_test, corange_test, core_left, core_right):
    points = strains.shape[2]
    chunks = points // CHUNK
    any_spec = pl.BlockSpec(memory_space=pl.ANY)
    dma = pltpu.SemaphoreType.DMA
    vmem = pltpu.VMEM
    own, range_all, core_all = pl.pallas_call(
        kernel,
        out_shape=(
            jax.ShapeDtypeStruct((64, points), F32),
            jax.ShapeDtypeStruct((16, 8, 256), F32),
            jax.ShapeDtypeStruct((16, 8, 16, 128), BF16),
        ),
        in_specs=[any_spec] * 6,
        out_specs=(any_spec,) * 3,
        scratch_shapes=[
            vmem((chunks, 6, 128, CHUNK), BF16),
            vmem((chunks, 2, CHUNK), F32),
            vmem((chunks, CHUNK, 256), BF16),
            vmem((chunks, 512, CHUNK), BF16),
            vmem((256, 128), BF16),
            vmem((512, 128), F32),
            vmem((128, CHUNK), BF16),
            vmem((512, 128), F32),
            vmem((128, 256), F32),
            vmem((chunks, 64, CHUNK), F32),
            vmem((chunks, 64, CHUNK), F32),
            vmem((chunks, 2, 64, CHUNK), BF16),
            vmem((chunks, 2, 64, CHUNK), BF16),
            vmem((chunks, 64, CHUNK), BF16),
            vmem((chunks, 64, CHUNK), BF16),
            vmem((16, 32, 128), BF16),
            vmem((15, 32, 128), BF16),
            vmem((15, 8, 256), F32),
            vmem((8, 256), F32),
            vmem((8, 256), F32),
            vmem((8, 256), F32),
            vmem((16, 8, 256), F32),
            vmem((8, 16, 128), F32),
            vmem((7, 16, 128), F32),
            vmem((16, 128), BF16),
            vmem((8, 16, 128), BF16),
            vmem((16, 8, 16, 128), BF16),
            dma((4, chunks)),
            dma((5,)),
            dma((chunks,)),
            dma((chunks,)),
            dma((chunks,)),
            dma((chunks,)),
            dma((4,)),
            dma((6,)),
            dma((4,)),
            dma((chunks + 2,)),
        ],
        compiler_params=pltpu.CompilerParams(collective_id=0, has_side_effects=True),
    )(strains, moduli, range_test, corange_test, core_left, core_right)
    core = core_all.reshape(16, 2, 4, 16, 128).transpose(2, 4, 0, 1, 3).reshape(512, 512)
    return range_all.reshape(128, 256), own, core.astype(F32)


def solution(mesh):
    in_specs = (
        P(None, "snap", "pts"),
        P(None, "pts"),
        P("pts", None),
        P(),
        P(None, "snap"),
        P(None, "pts"),
    )
    out_specs = (P("snap", None), P("snap", "pts"), P())
    return jax.shard_map(
        per_device, mesh=mesh, in_specs=in_specs, out_specs=out_specs, check_vma=False
    )
```

time: 557 us -> 49.5 us (0.09)
  the two profiles are of different devices: /device:TPU:0 before, /device:TPU:1 now
where the time goes in v1:
time: 49.5 us; the launch traced here: 49.4 us
  Pallas kernels  44.4 us (90%)
  local copies, waits for them, and re-layouts  4.35 us (9%)
  between operations  0.67 us (1%)
    pallas_call x1, Pallas kernels, per_device(): pl.pallas_call(kernel, out_shape=(jax.ShapeDtypeStruct((64, points), F32)...  44.4 us
    unnamed x8, local copies, waits for them, and re-layouts  3.01 us
    convert_element_type x1, local copies, waits for them, and re-layouts, per_device(): return (range_all.reshape(128, 256), own, core.astype(F32))  1.34 us

profile of v1, /device:TPU:1, one launch (start us, length us, event | category | flops | bytes accessed | tf_op | source)
XLA Modules:
  0.0 49.4 jit_solution(8281364056461317015)
XLA Ops:
  0.6 44.4 %shard_map.85 = (f32[64,4096]{1,0:T(8,128)}, f32[16,8,256]{2,1,0:T(8,128)}, bf16[16,8,16,128]{3,2,1,0:T(8,128)(2,1)}) custom-call(bf16[6,128,4096]{2,1,0:T(8,128)(2,1)} %strains_hbm.1, f32[2,4096]{1,0:T(2,128)} %moduli_hbm.1, bf16[4096,256]{1,0:T(8,128)(2,1)} %range_hbm.1, bf16[256,512]{1,0:T(8,128)(2,1)} %corange_hbm.1, f32[512,128]{1,0:T(8,128)} %left_hbm.1, ...), custom_call_target="tpu_custom_call" | custom-call | tf_op jit(solution)/shard_map/pallas_call | solution.py:379
  45.0 0.0 copy-start.1
  45.0 0.0 copy-start
  45.0 1.3 %copy.10 = f32[16,2,4,16,128]{4,2,3,1,0:T(4,128)S(1)} copy(bf16[16,2,4,16,128]{4,3,2,1,0:T(8,128)(2,1)} %bitcast.13) | data formatting | bytes 1572864 | tf_op jit(solution)/shard_map/convert_element_type | solution.py:430
  46.4 0.1 copy.14
  46.5 1.3 %copy.11 = f32[512,512]{1,0:T(8,128)} copy(f32[512,512]{0,1:T(8,128)S(1)} %bitcast.12) | data formatting | bytes 2097152
  47.8 0.0 copy-done.1
  47.8 0.7 %copy.17 = f32[128,256]{1,0:T(8,128)} copy(f32[128,256]{1,0:T(8,128)S(1)} %bitcast.14) | data formatting | bytes 262144
  48.4 0.0 copy-done
  48.4 1.0 %copy.18 = f32[64,4096]{1,0:T(8,128)} copy(f32[64,4096]{1,0:T(8,128)S(1)} %copy-done) | data formatting | bytes 2097152
Async XLA Ops:
  45.0 2.8 %copy-start.1 = (f32[16,8,256]{2,1,0:T(8,128)S(1)}, f32[16,8,256]{2,1,0:T(8,128)}, u32[]{:S(2)}) copy-start(f32[16,8,256]{2,1,0:T(8,128)} %get-tuple-element.6) | copy-start | bytes 393220
  45.0 3.4 %copy-start = (f32[64,4096]{1,0:T(8,128)S(1)}, f32[64,4096]{1,0:T(8,128)}, u32[]{:S(2)}) copy-start(f32[64,4096]{1,0:T(8,128)} %get-tuple-element.16) | copy-start | bytes 3145732

commit v2 on v0

v2 whole, which is shorter than its diff:
```python
import jax
import jax.numpy as jnp
from jax import lax
from jax.experimental import pallas as pl
from jax.experimental.pallas import tpu as pltpu
from jax.sharding import PartitionSpec as P

MESH = pl.DeviceIdType.MESH
F32 = jnp.float32
BF16 = jnp.bfloat16
NT = (((1,), (1,)), ((), ()))

CHUNK = 512
START = 3
HOLD = 3

ROOT = (
    0.5000000397996354,
    2 * 0.2499888951698186,
    -4 * 0.18699047969551208,
    8 * 0.24102109068796812,
    -16 * 0.3308495451729968,
    32 * 0.3494727775510849,
    -64 * 0.18534731636945423,
)
TINY = 1e-36


def hops(d):
    return sum(min(v, 4 - v) for v in d[:3])


OTHERS = sorted(
    (
        (dx, dy, dz, dc)
        for dx in range(4)
        for dy in range(4)
        for dz in range(4)
        for dc in range(2)
        if (dx, dy, dz, dc) != (0, 0, 0, 0)
    ),
    key=hops,
    reverse=True,
)
SAME_CORE = [d for d in OTHERS if d[3] == 0]
SAME_SNAP = [d for d in SAME_CORE if d[2] in (0, 2)]


def energy_tile(xx, yy, zz, xy, yz, xz, half_lame, shear):
    trace = xx + yy + zz
    mean = trace * (1.0 / 3.0)
    a = xx - mean
    b = yy - mean
    c = zz - mean
    ac = a * c
    d2 = xy * xy
    e2 = yz * yz
    f2 = xz * xz
    j2 = jnp.maximum((b * b - ac) + ((d2 + e2) + f2), TINY)
    half_det = 0.5 * (b * (ac - f2) - (a * e2 + c * d2)) + (xy * yz) * xz
    inv = lax.rsqrt(j2)
    ratio = (jnp.abs(half_det) * inv) * (inv * inv)
    root = jnp.full_like(ratio, ROOT[-1])
    for coef in ROOT[-2::-1]:
        root = root * ratio + coef
    outer = (j2 * inv) * root
    rest = jnp.maximum(j2 - 3.0 * (outer * outer), TINY)
    split = rest * lax.rsqrt(rest)
    outer = jnp.where(half_det < 0.0, -outer, outer)
    middle = mean - outer
    lone = jnp.maximum(mean + (outer + outer), 0.0)
    upper = jnp.maximum(middle + split, 0.0)
    lower = jnp.maximum(middle - split, 0.0)
    positive = jnp.maximum(trace, 0.0)
    squares = lone * lone + upper * upper + lower * lower
    return half_lame * (positive * positive) + shear * squares


def kernel(
    strains_hbm, moduli_hbm, range_hbm, corange_hbm, left_hbm, right_hbm,
    own_hbm, range_out_hbm, core_out_hbm,
    strains, moduli, range_w, right_w, corange_w, left_w, left_all, energy,
    cross_acc, range_acc, own_acc, far_acc, pair_send, pair_recv, far_send, far_recv,
    cross_send, cross_recv, range_send, range_recv, range_piece, range_all, range_sum,
    core_piece, core_all, order, core_sum,
    in_sems, w_sems, pair_ssem, pair_rsem, far_ssem, far_rsem,
    left_sems, cross_sems, range_sems, core_sems, out_sems,
):
    snap = lax.axis_index("snap")
    pts = lax.axis_index("pts")
    z_lo = snap // 2
    core = snap % 2
    z = pts // 16 * 2 + z_lo
    x = (pts // 4) % 4
    y = pts % 4

    def place(d):
        zz = (z + d[2]) % 4
        to_snap = zz % 2 * 2 + (core + d[3]) % 2
        return to_snap, zz // 2 * 16 + (x + d[0]) % 4 * 4 + (y + d[1]) % 4

    def device(where):
        return {"snap": where[0], "pts": where[1]}

    pair = (z_lo * 2 + (1 - core), pts)
    far_snap = (1 - z_lo) * 2 + core
    far = (far_snap, pts)
    outer_z = (z + 3 + 2 * z_lo) % 4
    outer = (far_snap, outer_z // 2 * 16 + pts % 16)

    def remote(src, dst, sems, send, recv, where):
        return pltpu.make_async_remote_copy(
            src_ref=src,
            dst_ref=dst,
            send_sem=sems.at[send],
            recv_sem=sems.at[recv],
            device_id=device(where),
            device_id_type=MESH,
        )

    chunks = strains.shape[0]

    def inputs(j):
        cols = pl.ds(pl.multiple_of(j * CHUNK, CHUNK), CHUNK)
        return (
            pltpu.make_async_copy(strains_hbm.at[:, :, cols], strains.at[j], in_sems.at[0, j]),
            pltpu.make_async_copy(moduli_hbm.at[:, cols], moduli.at[j], in_sems.at[1, j]),
            pltpu.make_async_copy(right_hbm.at[:, cols], right_w.at[j], in_sems.at[2, j]),
            pltpu.make_async_copy(range_hbm.at[cols, :], range_w.at[j], in_sems.at[3, j]),
        )

    weights = []
    own_cols = pl.ds(pl.multiple_of(snap * 128, 128), 128)
    pair_far = (1 - z_lo) * 2 + (1 - core)
    for n, owner in enumerate((snap, far_snap, pair[0], pair_far)):
        rows = pl.ds(pl.multiple_of(owner * 64, 64), 64)
        weights.append(
            pltpu.make_async_copy(
                corange_hbm.at[rows, own_cols], corange_w.at[pl.ds(n * 64, 64), :], w_sems.at[n]
            )
        )
    left_copy = pltpu.make_async_copy(left_hbm, left_w, w_sems.at[4])

    for copy in inputs(0):
        copy.start()
    left_copy.start()
    for copy in weights:
        copy.start()

    @pl.loop(1, chunks)
    def _(j):
        for copy in inputs(j):
            copy.start()

    barrier = pltpu.get_barrier_semaphore()
    me = snap * 32 + pts

    @pl.loop(1, 128)
    def _(n):
        other = (me + n) % 128
        pl.semaphore_signal(
            barrier, inc=1, device_id=device((other // 32, other % 32)), device_id_type=MESH
        )

    cross_acc[...] = jnp.zeros_like(cross_acc)
    range_acc[...] = jnp.zeros_like(range_acc)

    def pair_copy(j):
        return pltpu.make_async_remote_copy(
            src_ref=pair_send.at[j],
            dst_ref=pair_recv.at[j],
            send_sem=pair_ssem.at[j],
            recv_sem=pair_rsem.at[j],
            device_id=device(pair),
            device_id_type=MESH,
        )

    def far_copy(j):
        return pltpu.make_async_remote_copy(
            src_ref=far_send.at[j],
            dst_ref=far_recv.at[j],
            send_sem=far_ssem.at[j],
            recv_sem=far_rsem.at[j],
            device_id=device(far),
            device_id_type=MESH,
        )

    def pass_on(j):
        pair_copy(j).wait_recv()
        far_send[j] = (far_acc[j] + pair_recv[j, 1].astype(F32)).astype(BF16)
        far_copy(j).start()

    def energies(j):
        for lane in range(0, CHUNK, 128):
            cols = pl.ds(lane, 128)
            half_lame = 0.5 * moduli[j, 0:1, cols]
            shear = moduli[j, 1:2, cols]
            for row in range(0, 128, 16):
                rows = pl.ds(row, 16)
                parts = [strains[j, k, rows, cols].astype(F32) for k in range(6)]
                energy[j, rows, cols] = energy_tile(*parts, half_lame, shear).astype(BF16)

    def products(j):
        field = energy[j]
        own = jnp.dot(corange_w[...], field, preferred_element_type=F32)
        own_acc[j] = own[:64]
        far_acc[j] = own[64:128]
        pair_send[j, 0] = own[128:192].astype(BF16)
        pair_send[j, 1] = own[192:].astype(BF16)
        cross_acc[...] += lax.dot_general(right_w[j], field, NT, preferred_element_type=F32)
        range_acc[...] += jnp.dot(field, range_w[j], preferred_element_type=F32)

    def left_slot(s):
        return left_all.at[:, :, pl.ds(pl.multiple_of(s * 128, 128), 128)]

    def left_pair():
        return remote(left_slot(snap), left_slot(snap), left_sems, 0, 1, pair)

    def left_outer():
        return remote(left_slot(snap), left_slot(snap), left_sems, 2, 3, outer)

    def left_relay():
        return remote(left_slot(far_snap), left_slot(far_snap), left_sems, 4, 5, pair)

    for copy in inputs(0):
        copy.wait()
    energies(0)
    for copy in weights:
        copy.wait()
    left_copy.wait()
    left = left_w[...]
    left_top = left.astype(BF16)
    left_all[0, :, own_cols] = left_top
    left_all[1, :, own_cols] = (left - left_top.astype(F32)).astype(BF16)

    @pl.loop(1, chunks)
    def _(j):
        for copy in inputs(j):
            copy.wait()
        products(j - 1)
        energies(j)

        @pl.when(j == START)
        def _():
            pl.semaphore_wait(barrier, 127)
            left_outer().start()
            left_pair().start()
            for i in range(START - 1):
                pair_copy(i).start()

        @pl.when(j >= START)
        def _():
            pair_copy(j - 1).start()

        @pl.when((j > START) & (j <= START + HOLD))
        def _():
            pass_on(j - START - 1)

    products(chunks - 1)

    for n in range(128):
        cross_send[n] = cross_acc[pl.ds(n * 4, 4), :].astype(BF16)
    for d in OTHERS:
        where = place(d)
        remote(
            cross_send.at[where[0] * 32 + where[1]], cross_recv.at[snap, pts], cross_sems, 0, 1, where
        ).start()
    pltpu.make_async_copy(cross_send.at[me], cross_recv.at[snap, pts], cross_sems.at[1]).start()

    for n in range(32):
        rows, cols = pl.ds(n // 2 * 8, 8), pl.ds(n % 2 * 128, 128)
        range_send[n] = range_acc[rows, cols].astype(BF16)
    for d in SAME_SNAP:
        where = place(d)
        remote(range_send.at[where[1]], range_recv.at[pts], range_sems, 0, 1, where).start()
    pltpu.make_async_copy(range_send.at[pts], range_recv.at[pts], range_sems.at[1]).start()

    pair_copy(chunks - 1).start()
    done = min(HOLD, chunks - 1 - START)
    left_outer().wait_recv()
    left_relay().start()

    @pl.loop(done, chunks)
    def _(j):
        pass_on(j)

    row = lax.broadcasted_iota(jnp.int32, (512, 512), 0)
    col = lax.broadcasted_iota(jnp.int32, (512, 512), 1)
    source = (col & 127) // 4 * 16 + col // 128 * 4 + (col & 3)
    order[...] = jnp.where(row == source, 1.0, 0.0).astype(BF16)

    left_pair().wait_recv()
    left_relay().wait_recv()

    remote(cross_recv, cross_recv, cross_sems, 0, 1, pair).wait_recv()
    total = jnp.concatenate([jnp.sum(cross_recv[s].astype(F32), axis=0) for s in range(4)], axis=1)
    low = total - total.astype(BF16).astype(F32)
    both = jnp.concatenate([total, low], axis=0).astype(BF16)
    top = lax.dot_general(both, left_all[0], NT, preferred_element_type=F32)
    bottom = lax.dot_general(both, left_all[1], NT, preferred_element_type=F32)
    share = top[0:4] + (top[4:8] + bottom[0:4])
    core_piece[...] = jnp.concatenate(
        [share[:, k * 128 : k * 128 + 128] for k in range(4)], axis=0
    ).astype(BF16)
    slot = z_lo * 32 + pts
    for d in SAME_CORE:
        remote(core_piece, core_all.at[core, slot], core_sems, 0, 1, place(d)).start()
    pltpu.make_async_copy(core_piece, core_all.at[core, slot], core_sems.at[1]).start()

    remote(range_recv, range_recv, range_sems, 0, 1, pair).wait_recv()
    range_piece[...] = jnp.sum(range_recv[...].astype(F32), axis=0).astype(BF16)
    for d in SAME_SNAP:
        remote(range_piece, range_all.at[pts], range_sems, 2, 3, place(d)).start()
    pltpu.make_async_copy(range_piece, range_all.at[pts], range_sems.at[3]).start()

    def own_copy(j):
        cols = pl.ds(pl.multiple_of(j * CHUNK, CHUNK), CHUNK)
        return pltpu.make_async_copy(own_acc.at[j], own_hbm.at[:, cols], out_sems.at[j])

    @pl.loop(0, chunks)
    def _(j):
        far_copy(j).wait_recv()
        own_acc[j] = own_acc[j] + pair_recv[j, 0].astype(F32) + far_recv[j].astype(F32)
        own_copy(j).start()

    remote(core_all.at[core], core_all.at[core], core_sems, 0, 1, pair).wait_recv()
    relay = remote(core_all.at[core], core_all.at[core], core_sems, 2, 3, pair)
    relay.start()

    def arrange(which):
        for half in range(2):
            block = core_all[which, pl.ds(half * 32, 32)].reshape(512, 128)
            turned = lax.dot_general(
                block, order[...], (((0,), (0,)), ((), ())), preferred_element_type=F32
            ).astype(BF16)
            cols = pl.ds(pl.multiple_of((half * 2 + which) * 128, 128), 128)
            for k in range(4):
                core_sum[pl.ds(k * 128, 128), cols] = turned[:, k * 128 : k * 128 + 128]

    arrange(core)
    remote(range_all, range_all, range_sems, 2, 3, pair).wait_recv()
    for n in range(32):
        rows, cols = pl.ds(n // 2 * 8, 8), pl.ds(n % 2 * 128, 128)
        range_sum[rows, cols] = range_all[n].astype(F32)
    range_copy = pltpu.make_async_copy(range_sum, range_out_hbm, out_sems.at[chunks])
    range_copy.start()
    relay.wait_recv()
    arrange(1 - core)
    core_copy = pltpu.make_async_copy(core_sum, core_out_hbm, out_sems.at[chunks + 1])
    core_copy.start()

    left_outer().wait_send()
    left_pair().wait_send()
    left_relay().wait_send()
    sent = cross_send.at[pl.ds(0, 127)]
    remote(sent, sent, cross_sems, 0, 1, pair).wait_send()
    sent = range_send.at[pl.ds(0, 31)]
    remote(sent, sent, range_sems, 0, 1, pair).wait_send()
    remote(sent, sent, range_sems, 2, 3, pair).wait_send()
    sent = core_all.at[0, pl.ds(0, 63)]
    remote(sent, sent, core_sems, 0, 1, pair).wait_send()
    relay.wait_send()

    @pl.loop(0, chunks)
    def _(j):
        pair_copy(j).wait_send()
        far_copy(j).wait_send()
        own_copy(j).wait()

    range_copy.wait()
    core_copy.wait()


def per_device(strains, moduli, range_test, corange_test, core_left, core_right):
    points = strains.shape[2]
    chunks = points // CHUNK
    any_spec = pl.BlockSpec(memory_space=pl.ANY)
    dma = pltpu.SemaphoreType.DMA
    vmem = pltpu.VMEM
    own, range_sum, core = pl.pallas_call(
        kernel,
        out_shape=(
            jax.ShapeDtypeStruct((64, points), F32),
            jax.ShapeDtypeStruct((128, 256), F32),
            jax.ShapeDtypeStruct((512, 512), BF16),
        ),
        in_specs=[any_spec] * 6,
        out_specs=(any_spec,) * 3,
        scratch_shapes=[
            vmem((chunks, 6, 128, CHUNK), BF16),
            vmem((chunks, 2, CHUNK), F32),
            vmem((chunks, CHUNK, 256), BF16),
            vmem((chunks, 512, CHUNK), BF16),
            vmem((256, 128), BF16),
            vmem((512, 128), F32),
            vmem((2, 512, 512), BF16),
            vmem((chunks, 128, CHUNK), BF16),
            vmem((512, 128), F32),
            vmem((128, 256), F32),
            vmem((chunks, 64, CHUNK), F32),
            vmem((chunks, 64, CHUNK), F32),
            vmem((chunks, 2, 64, CHUNK), BF16),
            vmem((chunks, 2, 64, CHUNK), BF16),
            vmem((chunks, 64, CHUNK), BF16),
            vmem((chunks, 64, CHUNK), BF16),
            vmem((128, 4, 128), BF16),
            vmem((4, 32, 4, 128), BF16),
            vmem((32, 8, 128), BF16),
            vmem((32, 8, 128), BF16),
            vmem((8, 128), BF16),
            vmem((32, 8, 128), BF16),
            vmem((128, 256), F32),
            vmem((16, 128), BF16),
            vmem((2, 64, 16, 128), BF16),
            vmem((512, 512), BF16),
            vmem((512, 512), BF16),
            dma((4, chunks)),
            dma((5,)),
            dma((chunks,)),
            dma((chunks,)),
            dma((chunks,)),
            dma((chunks,)),
            dma((6,)),
            dma((2,)),
            dma((4,)),
            dma((4,)),
            dma((chunks + 2,)),
        ],
        compiler_params=pltpu.CompilerParams(collective_id=0, has_side_effects=True),
    )(strains, moduli, range_test, corange_test, core_left, core_right)
    return range_sum, own, core.astype(F32)


def solution(mesh):
    in_specs = (
        P(None, "snap", "pts"),
        P(None, "pts"),
        P("pts", None),
        P(),
        P(None, "snap"),
        P(None, "pts"),
    )
    out_specs = (P("snap", None), P("snap", "pts"), P())
    return jax.shard_map(
        per_device, mesh=mesh, in_specs=in_specs, out_specs=out_specs, check_vma=False
    )
```

time: 557 us -> 43.8 us (0.08)
  the two profiles are of different devices: /device:TPU:0 before, /device:TPU:1 now
where the time goes in v2:
time: 43.8 us; the launch traced here: 43.6 us
  Pallas kernels  37 us (84%)
  local copies, waits for them, and re-layouts  3.84 us (9%)
  other arithmetic  2.15 us (5%)
  between operations  0.64 us (1%)
    pallas_call x1, Pallas kernels, per_device(): pl.pallas_call(kernel, out_shape=(jax.ShapeDtypeStruct((64, points), F32)...  37 us
    unnamed x2, local copies, waits for them, and re-layouts  3.84 us
    convert_element_type x1, other arithmetic, per_device(): return (range_sum, own, core.astype(F32))  2.15 us

profile of v2, /device:TPU:1, one launch (start us, length us, event | category | flops | bytes accessed | tf_op | source)
XLA Modules:
  0.0 43.6 jit_solution(2260435978436420857)
XLA Ops:
  0.6 37.0 %shard_map.85 = (f32[64,4096]{1,0:T(8,128)}, f32[128,256]{1,0:T(8,128)}, bf16[512,512]{1,0:T(8,128)(2,1)}) custom-call(bf16[6,128,4096]{2,1,0:T(8,128)(2,1)} %strains_hbm.1, f32[2,4096]{1,0:T(2,128)} %moduli_hbm.1, bf16[4096,256]{1,0:T(8,128)(2,1)} %range_hbm.1, bf16[256,512]{1,0:T(8,128)(2,1)} %corange_hbm.1, f32[512,128]{1,0:T(8,128)} %left_hbm.1, ...), custom_call_target="tpu_custom_call" | custom-call | tf_op jit(solution)/shard_map/pallas_call | solution.py:380
  37.7 2.1 %convert_element_type.3 = f32[512,512]{1,0:T(8,128)} convert(bf16[512,512]{1,0:T(8,128)(2,1)} %get-tuple-element.8) | non-fusion elementwise | flops 262144 | bytes 1572864 | tf_op jit(solution)/shard_map/convert_element_type | solution.py:431
  39.8 1.6 %copy.11 = f32[128,256]{1,0:T(8,128)} copy(f32[128,256]{1,0:T(8,128)} %get-tuple-element.12) | data formatting | bytes 262144
  41.4 2.3 %copy.12 = f32[64,4096]{1,0:T(8,128)} copy(f32[64,4096]{1,0:T(8,128)} %get-tuple-element.13) | data formatting | bytes 2097152

commit v3 on v2

--- a/solution.py
+++ b/solution.py
@@ -12,7 +12,7 @@
 
 CHUNK = 512
 START = 3
-HOLD = 3
+CROSSING = (4, 4, 5, 6, 7, 8, 8, 8)
 
 ROOT = (
     0.5000000397996354,
@@ -78,13 +78,13 @@
 
 def kernel(
     strains_hbm, moduli_hbm, range_hbm, corange_hbm, left_hbm, right_hbm,
-    own_hbm, range_out_hbm, core_out_hbm,
+    own_acc, range_sum, core_sum,
     strains, moduli, range_w, right_w, corange_w, left_w, left_all, energy,
-    cross_acc, range_acc, own_acc, far_acc, pair_send, pair_recv, far_send, far_recv,
-    cross_send, cross_recv, range_send, range_recv, range_piece, range_all, range_sum,
-    core_piece, core_all, order, core_sum,
+    cross_acc, range_acc, far_acc, pair_send, pair_recv, far_send, far_recv,
+    cross_send, cross_recv, range_send, range_recv, range_piece, range_all,
+    core_piece, core_all, order,
     in_sems, w_sems, pair_ssem, pair_rsem, far_ssem, far_rsem,
-    left_sems, cross_sems, range_sems, core_sems, out_sems,
+    left_sems, cross_sems, range_sems, core_sems,
 ):
     snap = lax.axis_index("snap")
     pts = lax.axis_index("pts")
@@ -120,8 +120,11 @@
 
     chunks = strains.shape[0]
 
+    def columns(j):
+        return pl.ds(pl.multiple_of(j * CHUNK, CHUNK), CHUNK)
+
     def inputs(j):
-        cols = pl.ds(pl.multiple_of(j * CHUNK, CHUNK), CHUNK)
+        cols = columns(j)
         return (
             pltpu.make_async_copy(strains_hbm.at[:, :, cols], strains.at[j], in_sems.at[0, j]),
             pltpu.make_async_copy(moduli_hbm.at[:, cols], moduli.at[j], in_sems.at[1, j]),
@@ -200,14 +203,16 @@
                 parts = [strains[j, k, rows, cols].astype(F32) for k in range(6)]
                 energy[j, rows, cols] = energy_tile(*parts, half_lame, shear).astype(BF16)
 
-    def products(j):
+    def cross_product(j):
+        cross_acc[...] += lax.dot_general(right_w[j], energy[j], NT, preferred_element_type=F32)
+
+    def other_products(j):
         field = energy[j]
         own = jnp.dot(corange_w[...], field, preferred_element_type=F32)
-        own_acc[j] = own[:64]
+        own_acc[:, columns(j)] = own[:64]
         far_acc[j] = own[64:128]
         pair_send[j, 0] = own[128:192].astype(BF16)
         pair_send[j, 1] = own[192:].astype(BF16)
-        cross_acc[...] += lax.dot_general(right_w[j], field, NT, preferred_element_type=F32)
         range_acc[...] += jnp.dot(field, range_w[j], preferred_element_type=F32)
 
     def left_slot(s):
@@ -237,7 +242,8 @@
     def _(j):
         for copy in inputs(j):
             copy.wait()
-        products(j - 1)
+        other_products(j - 1)
+        cross_product(j - 1)
         energies(j)
 
         @pl.when(j == START)
@@ -252,11 +258,14 @@
         def _():
             pair_copy(j - 1).start()
 
-        @pl.when((j > START) & (j <= START + HOLD))
-        def _():
-            pass_on(j - START - 1)
-
-    products(chunks - 1)
+        for i, step in enumerate(CROSSING):
+            if step < chunks:
+
+                @pl.when(j == step)
+                def _(i=i):
+                    pass_on(i)
+
+    cross_product(chunks - 1)
 
     for n in range(128):
         cross_send[n] = cross_acc[pl.ds(n * 4, 4), :].astype(BF16)
@@ -267,6 +276,9 @@
         ).start()
     pltpu.make_async_copy(cross_send.at[me], cross_recv.at[snap, pts], cross_sems.at[1]).start()
 
+    other_products(chunks - 1)
+    pair_copy(chunks - 1).start()
+
     for n in range(32):
         rows, cols = pl.ds(n // 2 * 8, 8), pl.ds(n % 2 * 128, 128)
         range_send[n] = range_acc[rows, cols].astype(BF16)
@@ -275,14 +287,12 @@
         remote(range_send.at[where[1]], range_recv.at[pts], range_sems, 0, 1, where).start()
     pltpu.make_async_copy(range_send.at[pts], range_recv.at[pts], range_sems.at[1]).start()
 
-    pair_copy(chunks - 1).start()
-    done = min(HOLD, chunks - 1 - START)
     left_outer().wait_recv()
     left_relay().start()
 
-    @pl.loop(done, chunks)
-    def _(j):
-        pass_on(j)
+    for i, step in enumerate(CROSSING):
+        if step == chunks:
+            pass_on(i)
 
     row = lax.broadcasted_iota(jnp.int32, (512, 512), 0)
     col = lax.broadcasted_iota(jnp.int32, (512, 512), 1)
@@ -307,21 +317,23 @@
         remote(core_piece, core_all.at[core, slot], core_sems, 0, 1, place(d)).start()
     pltpu.make_async_copy(core_piece, core_all.at[core, slot], core_sems.at[1]).start()
 
+    for i, step in enumerate(CROSSING):
+        if step > chunks:
+            pass_on(i)
+
     remote(range_recv, range_recv, range_sems, 0, 1, pair).wait_recv()
     range_piece[...] = jnp.sum(range_recv[...].astype(F32), axis=0).astype(BF16)
     for d in SAME_SNAP:
         remote(range_piece, range_all.at[pts], range_sems, 2, 3, place(d)).start()
     pltpu.make_async_copy(range_piece, range_all.at[pts], range_sems.at[3]).start()
 
-    def own_copy(j):
-        cols = pl.ds(pl.multiple_of(j * CHUNK, CHUNK), CHUNK)
-        return pltpu.make_async_copy(own_acc.at[j], own_hbm.at[:, cols], out_sems.at[j])
-
     @pl.loop(0, chunks)
     def _(j):
         far_copy(j).wait_recv()
-        own_acc[j] = own_acc[j] + pair_recv[j, 0].astype(F32) + far_recv[j].astype(F32)
-        own_copy(j).start()
+        cols = columns(j)
+        own_acc[:, cols] = (
+            own_acc[:, cols] + pair_recv[j, 0].astype(F32) + far_recv[j].astype(F32)
+        )
 
     remote(core_all.at[core], core_all.at[core], core_sems, 0, 1, pair).wait_recv()
     relay = remote(core_all.at[core], core_all.at[core], core_sems, 2, 3, pair)
@@ -332,7 +344,7 @@
             block = core_all[which, pl.ds(half * 32, 32)].reshape(512, 128)
             turned = lax.dot_general(
                 block, order[...], (((0,), (0,)), ((), ())), preferred_element_type=F32
-            ).astype(BF16)
+            )
             cols = pl.ds(pl.multiple_of((half * 2 + which) * 128, 128), 128)
             for k in range(4):
                 core_sum[pl.ds(k * 128, 128), cols] = turned[:, k * 128 : k * 128 + 128]
@@ -342,12 +354,8 @@
     for n in range(32):
         rows, cols = pl.ds(n // 2 * 8, 8), pl.ds(n % 2 * 128, 128)
         range_sum[rows, cols] = range_all[n].astype(F32)
-    range_copy = pltpu.make_async_copy(range_sum, range_out_hbm, out_sems.at[chunks])
-    range_copy.start()
     relay.wait_recv()
     arrange(1 - core)
-    core_copy = pltpu.make_async_copy(core_sum, core_out_hbm, out_sems.at[chunks + 1])
-    core_copy.start()
 
     left_outer().wait_send()
     left_pair().wait_send()
@@ -365,10 +373,15 @@
     def _(j):
         pair_copy(j).wait_send()
         far_copy(j).wait_send()
-        own_copy(j).wait()
-
-    range_copy.wait()
-    core_copy.wait()
+
+
+def write_out(range_sum, own, core, range_out, own_out, core_out, sems):
+    pairs = ((core, core_out), (own, own_out), (range_sum, range_out))
+    copies = [pltpu.make_async_copy(a, b, sems.at[n]) for n, (a, b) in enumerate(pairs)]
+    for copy in copies:
+        copy.start()
+    for copy in copies:
+        copy.wait()
 
 
 def per_device(strains, moduli, range_test, corange_test, core_left, core_right):
@@ -377,15 +390,16 @@
     any_spec = pl.BlockSpec(memory_space=pl.ANY)
     dma = pltpu.SemaphoreType.DMA
     vmem = pltpu.VMEM
+    vmem_spec = pl.BlockSpec(memory_space=pltpu.VMEM)
     own, range_sum, core = pl.pallas_call(
         kernel,
         out_shape=(
-            jax.ShapeDtypeStruct((64, points), F32),
-            jax.ShapeDtypeStruct((128, 256), F32),
-            jax.ShapeDtypeStruct((512, 512), BF16),
+            vmem((64, points), F32),
+            vmem((128, 256), F32),
+            vmem((512, 512), F32),
         ),
         in_specs=[any_spec] * 6,
-        out_specs=(any_spec,) * 3,
+        out_specs=(vmem_spec,) * 3,
         scratch_shapes=[
             vmem((chunks, 6, 128, CHUNK), BF16),
             vmem((chunks, 2, CHUNK), F32),
@@ -398,7 +412,6 @@
             vmem((512, 128), F32),
             vmem((128, 256), F32),
             vmem((chunks, 64, CHUNK), F32),
-            vmem((chunks, 64, CHUNK), F32),
             vmem((chunks, 2, 64, CHUNK), BF16),
             vmem((chunks, 2, 64, CHUNK), BF16),
             vmem((chunks, 64, CHUNK), BF16),
@@ -409,10 +422,8 @@
             vmem((32, 8, 128), BF16),
             vmem((8, 128), BF16),
             vmem((32, 8, 128), BF16),
-            vmem((128, 256), F32),
             vmem((16, 128), BF16),
             vmem((2, 64, 16, 128), BF16),
-            vmem((512, 512), BF16),
             vmem((512, 512), BF16),
             dma((4, chunks)),
             dma((5,)),
@@ -424,11 +435,17 @@
             dma((2,)),
             dma((4,)),
             dma((4,)),
-            dma((chunks + 2,)),
         ],
         compiler_params=pltpu.CompilerParams(collective_id=0, has_side_effects=True),
     )(strains, moduli, range_test, corange_test, core_left, core_right)
-    return range_sum, own, core.astype(F32)
+    staged = [pltpu.with_memory_space_constraint(a, vmem) for a in (range_sum, own, core)]
+    return pl.pallas_call(
+        write_out,
+        out_shape=[jax.ShapeDtypeStruct(a.shape, F32) for a in (range_sum, own, core)],
+        in_specs=[vmem_spec] * 3,
+        out_specs=[any_spec] * 3,
+        scratch_shapes=[dma((3,))],
+    )(*staged)
 
 
 def solution(mesh):

time: 43.8 us -> 38.2 us (0.87)
  local copies, waits for them, and re-layouts: 3.84 us -> 0 us
  other arithmetic: 2.15 us -> 0 us
    unnamed x2 -> x0, local copies, waits for them, and re-layouts: 3.84 us -> none
    convert_element_type x1 -> x0, other arithmetic: 2.15 us -> none  [per_device(): return (range_sum, own, core.astype(F32))]
    pallas_call x1 -> x2, Pallas kernels: 37 us -> 37.4 us  [the longest x1 36.1 us: per_device(): pl.pallas_call(kernel, out_shape=(vmem((64, points), F32), vmem((128, 256...]
where the time goes in v3:
time: 38.2 us; the launch traced here: 38.1 us
  Pallas kernels  37.4 us (98%)
  between operations  0.64 us (2%)
    pallas_call x1, Pallas kernels, per_device(): pl.pallas_call(kernel, out_shape=(vmem((64, points), F32), vmem((128, 256...  36.1 us
    pallas_call x1, Pallas kernels, per_device(): pl.pallas_call(write_out, out_shape=[jax.ShapeDtypeStruct(a.shape, F32) f...  1.37 us

profile of v3, /device:TPU:1, one launch (start us, length us, event | category | flops | bytes accessed | tf_op | source)
XLA Modules:
  0.0 38.1 jit_solution(8194887748668893721)
XLA Ops:
  0.6 36.1 %shard_map.85 = (f32[64,4096]{1,0:T(8,128)S(1)}, f32[128,256]{1,0:T(8,128)S(1)}, f32[512,512]{1,0:T(8,128)S(1)}) custom-call(bf16[6,128,4096]{2,1,0:T(8,128)(2,1)} %strains_hbm.1, f32[2,4096]{1,0:T(2,128)} %moduli_hbm.1, bf16[4096,256]{1,0:T(8,128)(2,1)} %range_hbm.1, bf16[256,512]{1,0:T(8,128)(2,1)} %corange_hbm.1, f32[512,128]{1,0:T(8,128)} %left_hbm.1, ...), custom_call_target="tpu_custom_call" | custom-call | tf_op jit(solution)/shard_map/pallas_call | solution.py:394
  36.7 1.4 %shard_map.86 = (f32[128,256]{1,0:T(8,128)}, f32[64,4096]{1,0:T(8,128)}, f32[512,512]{1,0:T(8,128)}) custom-call(f32[128,256]{1,0:T(8,128)S(1)} %get-tuple-element.6.range_sum, f32[64,4096]{1,0:T(8,128)S(1)} %get-tuple-element.7.own, f32[512,512]{1,0:T(8,128)S(1)} %get-tuple-element.8.core), custom_call_target="tpu_custom_call" | custom-call | tf_op jit(solution)/shard_map/pallas_call | solution.py:442

commit v4 on v3

--- a/solution.py
+++ b/solution.py
@@ -11,8 +11,8 @@
 NT = (((1,), (1,)), ((), ()))
 
 CHUNK = 512
-START = 3
-CROSSING = (4, 4, 5, 6, 7, 8, 8, 8)
+START = 2
+CROSSING = (3, 3, 4, 5, 8, 8, 8, 8)
 
 ROOT = (
     0.5000000397996354,
@@ -79,7 +79,7 @@
 def kernel(
     strains_hbm, moduli_hbm, range_hbm, corange_hbm, left_hbm, right_hbm,
     own_acc, range_sum, core_sum,
-    strains, moduli, range_w, right_w, corange_w, left_w, left_all, energy,
+    strains, moduli, range_w, right_w, corange_w, left_w, left_all, energy_even, energy_odd,
     cross_acc, range_acc, far_acc, pair_send, pair_recv, far_send, far_recv,
     cross_send, cross_recv, range_send, range_recv, range_piece, range_all,
     core_piece, core_all, order,
@@ -121,7 +121,7 @@
     chunks = strains.shape[0]
 
     def columns(j):
-        return pl.ds(pl.multiple_of(j * CHUNK, CHUNK), CHUNK)
+        return pl.ds(j * CHUNK, CHUNK)
 
     def inputs(j):
         cols = columns(j)
@@ -150,8 +150,7 @@
     for copy in weights:
         copy.start()
 
-    @pl.loop(1, chunks)
-    def _(j):
+    for j in range(1, chunks):
         for copy in inputs(j):
             copy.start()
 
@@ -193,6 +192,8 @@
         far_send[j] = (far_acc[j] + pair_recv[j, 1].astype(F32)).astype(BF16)
         far_copy(j).start()
 
+    energy = (energy_even, energy_odd)
+
     def energies(j):
         for lane in range(0, CHUNK, 128):
             cols = pl.ds(lane, 128)
@@ -201,13 +202,13 @@
             for row in range(0, 128, 16):
                 rows = pl.ds(row, 16)
                 parts = [strains[j, k, rows, cols].astype(F32) for k in range(6)]
-                energy[j, rows, cols] = energy_tile(*parts, half_lame, shear).astype(BF16)
+                energy[j % 2][rows, cols] = energy_tile(*parts, half_lame, shear).astype(BF16)
 
     def cross_product(j):
-        cross_acc[...] += lax.dot_general(right_w[j], energy[j], NT, preferred_element_type=F32)
+        cross_acc[...] += lax.dot_general(right_w[j], energy[j % 2][...], NT, preferred_element_type=F32)
 
     def other_products(j):
-        field = energy[j]
+        field = energy[j % 2][...]
         own = jnp.dot(corange_w[...], field, preferred_element_type=F32)
         own_acc[:, columns(j)] = own[:64]
         far_acc[j] = own[64:128]
@@ -238,32 +239,23 @@
     left_all[0, :, own_cols] = left_top
     left_all[1, :, own_cols] = (left - left_top.astype(F32)).astype(BF16)
 
-    @pl.loop(1, chunks)
-    def _(j):
+    for j in range(1, chunks):
         for copy in inputs(j):
             copy.wait()
         other_products(j - 1)
         cross_product(j - 1)
         energies(j)
-
-        @pl.when(j == START)
-        def _():
+        if j == START:
             pl.semaphore_wait(barrier, 127)
             left_outer().start()
             left_pair().start()
             for i in range(START - 1):
                 pair_copy(i).start()
-
-        @pl.when(j >= START)
-        def _():
+        if j >= START:
             pair_copy(j - 1).start()
-
         for i, step in enumerate(CROSSING):
-            if step < chunks:
-
-                @pl.when(j == step)
-                def _(i=i):
-                    pass_on(i)
+            if step == j:
+                pass_on(i)
 
     cross_product(chunks - 1)
 
@@ -327,8 +319,7 @@
         remote(range_piece, range_all.at[pts], range_sems, 2, 3, place(d)).start()
     pltpu.make_async_copy(range_piece, range_all.at[pts], range_sems.at[3]).start()
 
-    @pl.loop(0, chunks)
-    def _(j):
+    for j in range(chunks):
         far_copy(j).wait_recv()
         cols = columns(j)
         own_acc[:, cols] = (
@@ -408,7 +399,8 @@
             vmem((256, 128), BF16),
             vmem((512, 128), F32),
             vmem((2, 512, 512), BF16),
-            vmem((chunks, 128, CHUNK), BF16),
+            vmem((128, CHUNK), BF16),
+            vmem((128, CHUNK), BF16),
             vmem((512, 128), F32),
             vmem((128, 256), F32),
             vmem((chunks, 64, CHUNK), F32),

time: 38.2 us -> 37.8 us (0.990)
  Pallas kernels: 37.4 us -> 37 us
    pallas_call x1, Pallas kernels: 36.1 us -> 35.7 us  [per_device(): pl.pallas_call(kernel, out_shape=(vmem((64, points), F32), vmem((128, 256...]
where the time goes in v4:
time: 37.8 us; the launch traced here: 37.7 us
  Pallas kernels  37 us (98%)
  between operations  0.64 us (2%)
    pallas_call x1, Pallas kernels, per_device(): pl.pallas_call(kernel, out_shape=(vmem((64, points), F32), vmem((128, 256...  35.7 us
    pallas_call x1, Pallas kernels, per_device(): pl.pallas_call(write_out, out_shape=[jax.ShapeDtypeStruct(a.shape, F32) f...  1.37 us

profile of v4, /device:TPU:1, one launch (start us, length us, event | category | flops | bytes accessed | tf_op | source)
XLA Modules:
  0.0 37.7 jit_solution(12906400197736301235)
XLA Ops:
  0.6 35.7 %shard_map.85 = (f32[64,4096]{1,0:T(8,128)S(1)}, f32[128,256]{1,0:T(8,128)S(1)}, f32[512,512]{1,0:T(8,128)S(1)}) custom-call(bf16[6,128,4096]{2,1,0:T(8,128)(2,1)} %strains_hbm.1, f32[2,4096]{1,0:T(2,128)} %moduli_hbm.1, bf16[4096,256]{1,0:T(8,128)(2,1)} %range_hbm.1, bf16[256,512]{1,0:T(8,128)(2,1)} %corange_hbm.1, f32[512,128]{1,0:T(8,128)} %left_hbm.1, ...), custom_call_target="tpu_custom_call" | custom-call | tf_op jit(solution)/shard_map/pallas_call | solution.py:385
  36.3 1.4 %shard_map.86 = (f32[128,256]{1,0:T(8,128)}, f32[64,4096]{1,0:T(8,128)}, f32[512,512]{1,0:T(8,128)}) custom-call(f32[128,256]{1,0:T(8,128)S(1)} %get-tuple-element.6.range_sum, f32[64,4096]{1,0:T(8,128)S(1)} %get-tuple-element.7.own, f32[512,512]{1,0:T(8,128)S(1)} %get-tuple-element.8.core), custom_call_target="tpu_custom_call" | custom-call | tf_op jit(solution)/shard_map/pallas_call | solution.py:434

commit v5 on v4

--- a/solution.py
+++ b/solution.py
@@ -205,7 +205,12 @@
                 energy[j % 2][rows, cols] = energy_tile(*parts, half_lame, shear).astype(BF16)
 
     def cross_product(j):
-        cross_acc[...] += lax.dot_general(right_w[j], energy[j % 2][...], NT, preferred_element_type=F32)
+        field = energy[j % 2][...]
+        for half in range(2):
+            rows = pl.ds(half * 256, 256)
+            cross_acc[rows, :] += lax.dot_general(
+                right_w[j, rows, :], field, NT, preferred_element_type=F32
+            )
 
     def other_products(j):
         field = energy[j % 2][...]
@@ -306,7 +311,7 @@
     ).astype(BF16)
     slot = z_lo * 32 + pts
     for d in SAME_CORE:
-        remote(core_piece, core_all.at[core, slot], core_sems, 0, 1, place(d)).start()
+        remote(core_piece, core_all.at[core, slot], core_sems, 0, 1 + d[2] % 2, place(d)).start()
     pltpu.make_async_copy(core_piece, core_all.at[core, slot], core_sems.at[1]).start()
 
     for i, step in enumerate(CROSSING):
@@ -326,27 +331,41 @@
             own_acc[:, cols] + pair_recv[j, 0].astype(F32) + far_recv[j].astype(F32)
         )
 
-    remote(core_all.at[core], core_all.at[core], core_sems, 0, 1, pair).wait_recv()
-    relay = remote(core_all.at[core], core_all.at[core], core_sems, 2, 3, pair)
-    relay.start()
-
-    def arrange(which):
-        for half in range(2):
-            block = core_all[which, pl.ds(half * 32, 32)].reshape(512, 128)
-            turned = lax.dot_general(
-                block, order[...], (((0,), (0,)), ((), ())), preferred_element_type=F32
-            )
-            cols = pl.ds(pl.multiple_of((half * 2 + which) * 128, 128), 128)
-            for k in range(4):
-                core_sum[pl.ds(k * 128, 128), cols] = turned[:, k * 128 : k * 128 + 128]
-
-    arrange(core)
+    def half_of(which, half):
+        return core_all.at[which, pl.ds(pl.multiple_of(half * 32, 32), 32)]
+
+    def arrived(half, recv):
+        ref = half_of(core, half)
+        remote(ref, ref, core_sems, 0, recv, pair).wait_recv()
+
+    def relay(half, n):
+        ref = half_of(core, half)
+        return remote(ref, ref, core_sems, 3 + n, 5 + n, pair)
+
+    def arrange(which, half):
+        block = half_of(which, half)[...].reshape(512, 128)
+        turned = lax.dot_general(
+            block, order[...], (((0,), (0,)), ((), ())), preferred_element_type=F32
+        )
+        cols = pl.ds(pl.multiple_of((half * 2 + which) * 128, 128), 128)
+        for k in range(4):
+            core_sum[pl.ds(k * 128, 128), cols] = turned[:, k * 128 : k * 128 + 128]
+
+    first, second = 1 - z_lo, z_lo
+    arrived(first, 2)
+    relay(first, 0).start()
+    arrange(core, first)
+    arrived(second, 1)
+    relay(second, 1).start()
+    arrange(core, second)
     remote(range_all, range_all, range_sems, 2, 3, pair).wait_recv()
     for n in range(32):
         rows, cols = pl.ds(n // 2 * 8, 8), pl.ds(n % 2 * 128, 128)
         range_sum[rows, cols] = range_all[n].astype(F32)
-    relay.wait_recv()
-    arrange(1 - core)
+    relay(first, 0).wait_recv()
+    arrange(1 - core, first)
+    relay(second, 1).wait_recv()
+    arrange(1 - core, second)
 
     left_outer().wait_send()
     left_pair().wait_send()
@@ -358,7 +377,8 @@
     remote(sent, sent, range_sems, 2, 3, pair).wait_send()
     sent = core_all.at[0, pl.ds(0, 63)]
     remote(sent, sent, core_sems, 0, 1, pair).wait_send()
-    relay.wait_send()
+    relay(first, 0).wait_send()
+    relay(second, 1).wait_send()
 
     @pl.loop(0, chunks)
     def _(j):
@@ -426,7 +446,7 @@
             dma((6,)),
             dma((2,)),
             dma((4,)),
-            dma((4,)),
+            dma((7,)),
         ],
         compiler_params=pltpu.CompilerParams(collective_id=0, has_side_effects=True),
     )(strains, moduli, range_test, corange_test, core_left, core_right)

time: 37.8 us -> 37.5 us (level)
  no operation moved by 1% of the time
where the time goes in v5:
time: 37.5 us; the launch traced here: 37.4 us
  Pallas kernels  36.8 us (98%)
  between operations  0.64 us (2%)
    pallas_call x1, Pallas kernels, per_device(): pl.pallas_call(kernel, out_shape=(vmem((64, points), F32), vmem((128, 256...  35.4 us
    pallas_call x1, Pallas kernels, per_device(): pl.pallas_call(write_out, out_shape=[jax.ShapeDtypeStruct(a.shape, F32) f...  1.37 us

profile of v5, /device:TPU:1, one launch (start us, length us, event | category | flops | bytes accessed | tf_op | source)
XLA Modules:
  0.0 37.4 jit_solution(5038725431603081265)
XLA Ops:
  0.6 35.4 %shard_map.85 = (f32[64,4096]{1,0:T(8,128)S(1)}, f32[128,256]{1,0:T(8,128)S(1)}, f32[512,512]{1,0:T(8,128)S(1)}) custom-call(bf16[6,128,4096]{2,1,0:T(8,128)(2,1)} %strains_hbm.1, f32[2,4096]{1,0:T(2,128)} %moduli_hbm.1, bf16[4096,256]{1,0:T(8,128)(2,1)} %range_hbm.1, bf16[256,512]{1,0:T(8,128)(2,1)} %corange_hbm.1, f32[512,128]{1,0:T(8,128)} %left_hbm.1, ...), custom_call_target="tpu_custom_call" | custom-call | tf_op jit(solution)/shard_map/pallas_call | solution.py:405
  36.0 1.4 %shard_map.86 = (f32[128,256]{1,0:T(8,128)}, f32[64,4096]{1,0:T(8,128)}, f32[512,512]{1,0:T(8,128)}) custom-call(f32[128,256]{1,0:T(8,128)S(1)} %get-tuple-element.6.range_sum, f32[64,4096]{1,0:T(8,128)S(1)} %get-tuple-element.7.own, f32[512,512]{1,0:T(8,128)S(1)} %get-tuple-element.8.core), custom_call_target="tpu_custom_call" | custom-call | tf_op jit(solution)/shard_map/pallas_call | solution.py:454
